TPU v7x, 32 devices: a whole 2x2x4 slice. The times are simulated.
32 devices in a mesh: conv: 4 (over y, core), seq: 4 (over z), tensor: 2 (over x).
Axes of the slice: x: 2, y: 2, z: 4, core: 2. Of those that a mesh axis runs over, the one named last changes fastest.
Arguments:
- queries: bfloat16 [4, 512, 4096], P('conv', 'seq', 'tensor'), may hold values from -6 to 6
- keys: bfloat16 [8, 1664, 1024], P('conv', ('seq', 'tensor')), may hold values from -6 to 6
- values: bfloat16 [8, 1664, 1024], P('conv', ('seq', 'tensor')), may hold values from -18 to 18
- q_gain: float32 [128], replicated, may hold values from 0.9 to 2.2
- k_gain: float32 [128], replicated, may hold values from 0.9 to 2.2
- gate: float32 [1], replicated, may hold values from 0.4 to 1.6
- tile_count: int32 [4], replicated, may hold values from 1 to 2, as said below
- tile_owner: int32 [4, 2], replicated, may hold values from -1 to 3, as said below
- visible: int32 [4, 512], replicated, may hold values from 0 to 2, as said below
- d_out: bfloat16 [4, 512, 4096], P('conv', 'seq', 'tensor'), may hold values from -12 to 12
Outputs:
- attended: bfloat16 [4, 512, 4096], P('conv', 'seq', 'tensor')
- d_queries: bfloat16 [4, 512, 4096], P('conv', 'seq', 'tensor')
- d_keys: bfloat16 [8, 1664, 1024], P('conv', ('seq', 'tensor'))
- d_values: bfloat16 [8, 1664, 1024], P('conv', ('seq', 'tensor'))
Inputs may be any that keep to these rules, and one draw needn't show every extreme that they name: `tile_count`: some conversation has 2 tiles. `tile_owner`: entries with t at or past the conversation's count are -1. The tiles of one conversation have different owners, no two tiles share a slot, and some conv index holds 2 tiles. `visible`: never falls along a conversation's text; it is 0 at the first token and 2 at the last.
All inputs are finite; a program needn't handle non-finite values.
Results may differ from a plain program's by a relative error of at most 0.02.
Values may be sent and summed in bfloat16 or wider, within the bound.
A program may use at most 128 MiB of HBM per device.

v0:
```python
from functools import partial
import math
import jax
import jax.numpy as jnp
from jax import lax
from jax.sharding import PartitionSpec as P

TILE = 1601
EPSILON = 1e-05


def head_norm(inputs, norm_gain):
    mean_square = jnp.mean(inputs * inputs, axis=-1, keepdims=True)
    return inputs * lax.rsqrt(mean_square + EPSILON) * norm_gain


def key_mask(seen_tiles, tile_index, row_start, row_count):
    row_ids = row_start + jnp.arange(row_count, dtype=jnp.int32)
    return (seen_tiles > tile_index)[:, None] & (row_ids < TILE)[None, :]


def tile_weights(query_bf, key_tile, visible_keys, score_scale):
    scores = (
        jnp.einsum("pkgd,rkd->kgpr", query_bf, key_tile, preferred_element_type=jnp.float32)
        * score_scale
    )
    return jnp.where(visible_keys[None, None], jnp.exp(scores), 0.0)


def tile_forward(query_bf, key_tile, value_tile, visible_keys, score_scale):
    weights = tile_weights(query_bf, key_tile, visible_keys, score_scale)
    weighted = jnp.einsum(
        "kgpr,rkd->pkgd",
        weights.astype(jnp.bfloat16),
        value_tile,
        preferred_element_type=jnp.float32,
    )
    return (jnp.sum(weights, axis=-1), weighted)


def tile_gradients(
    query_bf,
    grad_bf,
    key_tile,
    value_tile,
    visible_keys,
    safe_sum,
    row_delta,
    score_scale,
    block_count,
):
    weights = tile_weights(query_bf, key_tile, visible_keys, score_scale)
    probability = weights / safe_sum[..., None]
    grad_prob = jnp.einsum(
        "pkgd,rkd->kgpr", grad_bf, value_tile, preferred_element_type=jnp.float32
    )
    grad_score = (probability * (grad_prob - row_delta[..., None])).astype(jnp.bfloat16)
    prob_bf = probability.astype(jnp.bfloat16)
    grad_query = (
        jnp.einsum("kgpr,rkd->pkgd", grad_score, key_tile, preferred_element_type=jnp.float32)
        * score_scale
    )
    kv_local, group_size, token_count, row_count = grad_score.shape
    head_size = query_bf.shape[-1]
    block_tokens = token_count // block_count
    score_blocks = grad_score.reshape(kv_local, group_size, block_count, block_tokens, row_count)
    prob_blocks = prob_bf.reshape(kv_local, group_size, block_count, block_tokens, row_count)
    query_blocks = query_bf.reshape(block_count, block_tokens, kv_local, group_size, head_size)
    grad_blocks = grad_bf.reshape(block_count, block_tokens, kv_local, group_size, head_size)
    key_part = (
        jnp.einsum(
            "kgbpr,bpkgd->brkd", score_blocks, query_blocks, preferred_element_type=jnp.float32
        )
        * score_scale
    )
    value_part = jnp.einsum(
        "kgbpr,bpkgd->brkd", prob_blocks, grad_blocks, preferred_element_type=jnp.float32
    )
    key_part = jnp.sum(
        lax.optimization_barrier(key_part.astype(jnp.bfloat16)).astype(jnp.float32), axis=0
    )
    value_part = jnp.sum(
        lax.optimization_barrier(value_part.astype(jnp.bfloat16)).astype(jnp.float32), axis=0
    )
    return (
        grad_query,
        key_part.reshape(row_count, kv_local * head_size),
        value_part.reshape(row_count, kv_local * head_size),
    )


def attend_forward(query_bf, tile_keys, tile_values, seen_tiles, row_start, score_scale):
    row_count, slot_count, features = tile_keys.shape
    token_count, kv_local, group_size, head_size = query_bf.shape
    weight_sum = jnp.zeros((kv_local, group_size, token_count), jnp.float32)
    weighted = jnp.zeros(query_bf.shape, jnp.float32)
    for tile_index in range(slot_count):
        key_tile = tile_keys[:, tile_index].reshape(row_count, kv_local, head_size)
        value_tile = tile_values[:, tile_index].reshape(row_count, kv_local, head_size)
        visible_keys = key_mask(seen_tiles, tile_index, row_start, row_count)
        work = partial(tile_forward, query_bf, key_tile, value_tile, visible_keys, score_scale)
        part_sum, part_weighted = work()
        weight_sum = weight_sum + part_sum
        weighted = weighted + part_weighted
    return (weight_sum, weighted)


def attend_backward(
    query_bf,
    grad_bf,
    tile_keys,
    tile_values,
    seen_tiles,
    row_start,
    safe_sum,
    row_delta,
    score_scale,
    block_tokens,
):
    row_count, slot_count, features = tile_keys.shape
    token_count, kv_local, group_size, head_size = query_bf.shape
    block_count = token_count // block_tokens
    grad_query = jnp.zeros(query_bf.shape, jnp.float32)
    key_parts = []
    value_parts = []
    for tile_index in range(slot_count):
        key_tile = tile_keys[:, tile_index].reshape(row_count, kv_local, head_size)
        value_tile = tile_values[:, tile_index].reshape(row_count, kv_local, head_size)
        visible_keys = key_mask(seen_tiles, tile_index, row_start, row_count)
        work = partial(
            tile_gradients,
            query_bf,
            grad_bf,
            key_tile,
            value_tile,
            visible_keys,
            safe_sum,
            row_delta,
            score_scale,
            block_count,
        )
        part_query, key_part, value_part = work()
        grad_query = grad_query + part_query
        key_parts.append(key_part)
        value_parts.append(value_part)
    return (grad_query, jnp.stack(key_parts, axis=1), jnp.stack(value_parts, axis=1))


def shards(queries, keys, values, q_gain, k_gain, gate, tile_count, tile_owner, visible, d_out):
    conv_count = lax.axis_size("conv")
    tensor_count = lax.axis_size("tensor")
    conv_index = lax.axis_index("conv")
    sequence_index = lax.axis_index("seq")
    slot_count, row_local, features = keys.shape
    head_size = q_gain.shape[0]
    kv_heads = features // head_size
    kv_local = kv_heads // tensor_count
    token_count = queries.shape[1]
    query_heads = queries.shape[2] // head_size
    group_size = query_heads // kv_local
    score_scale = 1.0 / math.sqrt(head_size)
    gate_value = jnp.tanh(gate[0])
    conv_ids = jnp.arange(conv_count, dtype=jnp.int32)
    transfers = (tile_owner == conv_index).astype(jnp.bfloat16)
    own_owners = lax.dynamic_index_in_dim(tile_owner, conv_index, 0, keepdims=False)
    takes = (own_owners[:, None] == conv_ids[None, :]).astype(jnp.bfloat16)
    own_count = lax.dynamic_index_in_dim(tile_count, conv_index, 0, keepdims=False)
    seen_all = jnp.minimum(
        lax.dynamic_index_in_dim(visible, conv_index, 0, keepdims=False), own_count
    )
    key_raw = keys.astype(jnp.float32).reshape(slot_count, row_local, kv_heads, head_size)
    key_normed, key_back = jax.vjp(lambda inputs: head_norm(inputs, k_gain), key_raw)
    key_halfprec = key_normed.astype(jnp.bfloat16).reshape(slot_count, row_local, features)
    outgoing_keys = jnp.einsum(
        "wn,nki->wki", transfers, key_halfprec, preferred_element_type=jnp.float32
    ).astype(jnp.bfloat16)
    send_values = jnp.einsum(
        "wn,nki->wki", transfers, values, preferred_element_type=jnp.float32
    ).astype(jnp.bfloat16)
    got_keys, got_values = (
        lax.all_to_all(
            lax.all_to_all(outgoing_keys, "conv", split_axis=0, concat_axis=0, tiled=True),
            "tensor",
            split_axis=2,
            concat_axis=1,
            tiled=True,
        ),
        lax.all_to_all(
            lax.all_to_all(send_values, "conv", split_axis=0, concat_axis=0, tiled=True),
            "tensor",
            split_axis=2,
            concat_axis=1,
            tiled=True,
        ),
    )
    tile_keys = jnp.einsum(
        "to,orf->rtf", takes, got_keys, preferred_element_type=jnp.float32
    ).astype(jnp.bfloat16)
    tile_values = jnp.einsum(
        "to,orf->rtf", takes, got_values, preferred_element_type=jnp.float32
    ).astype(jnp.bfloat16)
    query_raw = queries[0].astype(jnp.float32).reshape(token_count, query_heads, head_size)
    query_normed, query_back = jax.vjp(lambda inputs: head_norm(inputs, q_gain), query_raw)
    query_bf = query_normed.astype(jnp.bfloat16).reshape(
        token_count, kv_local, group_size, head_size
    )
    grad_bf = (
        (gate_value * d_out[0].astype(jnp.float32))
        .astype(jnp.bfloat16)
        .reshape(token_count, kv_local, group_size, head_size)
    )
    own_start = sequence_index * token_count
    all_queries = lax.all_gather(query_bf, "seq", axis=0, tiled=True)
    all_grads = lax.all_gather(grad_bf, "seq", axis=0, tiled=True)
    share_rows = tile_keys.shape[0]
    row_start = sequence_index * share_rows
    part_sum, part_weighted = attend_forward(
        all_queries, tile_keys, tile_values, seen_all, row_start, score_scale
    )
    all_weighted, all_weight_sum = (
        lax.psum(part_weighted.astype(jnp.bfloat16), "seq").astype(jnp.float32),
        lax.psum(part_sum.astype(jnp.bfloat16), "seq").astype(jnp.float32),
    )
    safe_all = jnp.where(all_weight_sum > 0, all_weight_sum, 1.0)
    context_all = all_weighted / jnp.transpose(safe_all, (2, 0, 1))[..., None]
    context = lax.dynamic_slice_in_dim(context_all, own_start, token_count, 0)
    row_delta = jnp.transpose(
        jnp.sum(all_grads.astype(jnp.float32) * context_all, axis=-1), (1, 2, 0)
    )
    grad_part, key_sums, value_sums = attend_backward(
        all_queries,
        all_grads,
        tile_keys,
        tile_values,
        seen_all,
        row_start,
        safe_all,
        row_delta,
        score_scale,
        token_count,
    )
    grad_query = lax.psum_scatter(
        grad_part.astype(jnp.bfloat16), "seq", scatter_dimension=0, tiled=True
    ).astype(jnp.float32)
    attended = (
        (gate_value * context).astype(jnp.bfloat16).reshape(1, token_count, query_heads * head_size)
    )
    key_round = key_sums.astype(jnp.bfloat16)
    value_round = value_sums.astype(jnp.bfloat16)
    back_keys = jnp.einsum(
        "to,rtf->orf", takes, key_round, preferred_element_type=jnp.float32
    ).astype(jnp.bfloat16)
    back_values = jnp.einsum(
        "to,rtf->orf", takes, value_round, preferred_element_type=jnp.float32
    ).astype(jnp.bfloat16)
    returned_keys, returned_values = (
        lax.all_to_all(
            lax.all_to_all(back_keys, "conv", split_axis=0, concat_axis=0, tiled=True),
            "tensor",
            split_axis=1,
            concat_axis=2,
            tiled=True,
        ),
        lax.all_to_all(
            lax.all_to_all(back_values, "conv", split_axis=0, concat_axis=0, tiled=True),
            "tensor",
            split_axis=1,
            concat_axis=2,
            tiled=True,
        ),
    )
    positioned_keys = jnp.einsum(
        "ew,eig->wig", transfers, returned_keys, preferred_element_type=jnp.float32
    )
    d_values = jnp.einsum(
        "ew,eig->wig", transfers, returned_values, preferred_element_type=jnp.float32
    ).astype(jnp.bfloat16)
    d_keys = key_back(positioned_keys.reshape(slot_count, row_local, kv_heads, head_size))[0]
    d_keys = d_keys.astype(jnp.bfloat16).reshape(slot_count, row_local, features)
    d_queries = query_back(grad_query.reshape(token_count, query_heads, head_size))[0]
    d_queries = d_queries.astype(jnp.bfloat16).reshape(1, token_count, query_heads * head_size)
    return (attended, d_queries, d_keys, d_values)


def solution(mesh):
    in_specs = (
        P("conv", "seq", "tensor"),
        P("conv", ("seq", "tensor"), None),
        P("conv", ("seq", "tensor"), None),
        P(),
        P(),
        P(),
        P(),
        P(),
        P(),
        P("conv", "seq", "tensor"),
    )
    out_specs = (
        P("conv", "seq", "tensor"),
        P("conv", "seq", "tensor"),
        P("conv", ("seq", "tensor"), None),
        P("conv", ("seq", "tensor"), None),
    )
    return jax.shard_map(shards, mesh=mesh, in_specs=in_specs, out_specs=out_specs, check_vma=False)
```

profile of v0, /device:TPU:0, one launch (start us, length us, event | category | flops | bytes accessed | tf_op | source)
XLA Modules:
  0.0 426.6 jit_solution(4525607871681992089)
XLA Ops:
  18.6 4.4 %all-to-all-start.2 = ((bf16[4,208,1024]{2,1,0:T(8,128)(2,1)}), bf16[4,208,1024]{2,1,0:T(8,128)(2,1)}, u32[]{:S(2)}, u32[]{:S(2)}) async-start(bf16[4,208,1024]{2,1,0:T(8,128)(2,1)} %copy.195), calls=%async_computation.2 | async-start | bytes 3407872 | tf_op jit(solution)/shard_map/all_to_all | solution.py:182
  29.1 16.1 %all-to-all-done.2 = bf16[4,208,1024]{2,1,0:T(8,128)(2,1)} async-done(((bf16[4,208,1024]{2,1,0:T(8,128)(2,1)}), bf16[4,208,1024]{2,1,0:T(8,128)(2,1)}, u32[]{:S(2)}, u32[]{:S(2)}) %all-to-all-start.2) | async-done | bytes 1703968 | tf_op jit(solution)/shard_map/all_to_all | solution.py:182
  48.7 4.2 copy.196
  53.0 17.2 %all-to-all-done = bf16[4,208,1024]{2,1,0:T(8,128)(2,1)S(1)} async-done(((bf16[4,208,1024]{2,1,0:T(8,128)(2,1)}), bf16[4,208,1024]{2,1,0:T(8,128)(2,1)S(1)}, u32[]{:S(2)}, u32[]{:S(2)}) %all-to-all-start) | async-done | bytes 1703968 | tf_op jit(solution)/shard_map/all_to_all | solution.py:189
  79.2 4.2 copy.190
  83.4 17.2 %all-to-all-done.3 = bf16[4,208,1024]{1,0,2:T(4,128)(2,1)S(1)} async-done(((bf16[4,208,1024]{1,0,2:T(4,128)(2,1)}), bf16[4,208,1024]{1,0,2:T(4,128)(2,1)S(1)}, u32[]{:S(2)}, u32[]{:S(2)}) %all-to-all-start.3) | async-done | bytes 1703968 | tf_op jit(solution)/shard_map/all_to_all | solution.py:181
  100.6 4.8 %all-to-all-start.1 = ((bf16[4,208,1024]{1,0,2:T(4,128)(2,1)}), bf16[4,208,1024]{1,0,2:T(4,128)(2,1)}, u32[]{:S(2)}, u32[]{:S(2)}) async-start(bf16[4,208,1024]{1,0,2:T(4,128)(2,1)} %copy.190), calls=%async_computation.1 | async-start | bytes 4194304 | tf_op jit(solution)/shard_map/all_to_all | solution.py:188
  105.9 3.9 copy.197
  117.9 12.1 %all-to-all-done.1 = bf16[4,208,1024]{1,0,2:T(4,128)(2,1)} async-done(((bf16[4,208,1024]{1,0,2:T(4,128)(2,1)}), bf16[4,208,1024]{1,0,2:T(4,128)(2,1)}, u32[]{:S(2)}, u32[]{:S(2)}) %all-to-all-start.1) | async-done | bytes 1703968 | tf_op jit(solution)/shard_map/all_to_all | solution.py:188
  129.9 5.4 %copy.191 = bf16[4,208,2,512]{3,0,1,2:T(4,128)(2,1)S(1)} copy(bf16[4,208,2,512]{1,0,3,2:T(4,128)(2,1)} %bitcast.2) | data formatting | bytes 3407872 | tf_op jit(solution)/shard_map/all_to_all | solution.py:188
  140.4 8.4 %fusion.8 = (f32[4,4,512]{2,1,0:T(4,128)S(1)}, f32[4,416,512,4]{2,1,3,0:T(8,128)}) fusion(pred[512,416]{0,1:T(8,128)(4,1)S(1)} %get-tuple-element.37, bf16[512,4,4,128]{3,0,2,1:T(8,128)(2,1)} %all-gather.3.cloned.1.call-done, bf16[416,4,128,1]{2,1,0,3:T(4,128)(2,1)S(1)} %bitcast.268), kind=kOutput, calls=%fused_computation.12 | convolution fusion | flops 882630656 | bytes 16400384 | tf_op jit(solution)/shard_map/pkgd,rkd->kgpr/dot_general | solution.py:24
  148.8 6.6 %fusion.5 = (f32[4,4,512]{2,1,0:T(4,128)S(1)}, f32[4,416,512,4]{2,1,3,0:T(8,128)}) fusion(pred[512,416]{0,1:T(8,128)(4,1)S(1)} %get-tuple-element.36, bf16[512,4,4,128]{3,0,2,1:T(8,128)(2,1)S(1)} %copy-done.38, bf16[416,4,128,1]{2,1,0,3:T(4,128)(2,1)S(1)} %bitcast.270), kind=kOutput, calls=%fused_computation.9 | convolution fusion | flops 882630656 | bytes 16400384 | tf_op jit(solution)/shard_map/pkgd,rkd->kgpr/dot_general | solution.py:24
  155.5 19.6 %psum.15 = bf16[4,4,512]{2,1,0:T(4,128)(2,1)S(1)} all-reduce(bf16[4,4,512]{2,1,0:T(4,128)(2,1)S(1)} %add_convert_fusion.1), channel_id=1, replica_groups=mesh['conv'=4,'seq'=4,'tensor'=2] {'seq'}, use_global_device_ids=true, to_apply=%region_5.6 | all-reduce | flops 8192 | bytes 32768 | tf_op jit(solution)/shard_map/psum | solution.py:222
  175.0 6.4 %fusion.10 = f32[4,128,4,512]{3,1,2,0:T(8,128)S(1)} fusion(f32[4,416,512,4]{2,1,3,0:T(8,128)} %get-tuple-element.41, pred[512,416]{0,1:T(8,128)(4,1)S(1)} %get-tuple-element.37, bf16[416,4,128,1]{2,1,0,3:T(4,128)(2,1)S(1)} %bitcast.262), kind=kOutput, calls=%fused_computation.14 | convolution fusion | flops 882638848 | bytes 18464768 | tf_op jit(solution)/shard_map/kgpr,rkd->pkgd/dot_general | solution.py:32
  187.7 15.6 %convert_bitcast_fusion.1 = (bf16[4,4,52,4,8,128]{5,4,3,2,1,0:T(8,128)(2,1)}, bf16[4,4,52,4,8,128]{5,4,3,2,1,0:T(8,128)(2,1)}) fusion(f32[4,4,512]{2,1,0:T(4,128)S(1)} %get-tuple-element.34, f32[4,416,512,4]{2,1,3,0:T(8,128)} %get-tuple-element.39, pred[512,416]{0,1:T(8,128)(4,1)S(1)} %get-tuple-element.36, f32[4,416,512,4]{2,1,3,0:T(8,128)} %get-tuple-element.41, ...), kind=kLoop, calls=%fused_computation.29 | loop fusion | flops 27262976 | bytes 41353216
  208.5 6.7 %fusion.62 = bf16[4,416,4,128]{3,1,2,0:T(8,128)(2,1)} fusion(bf16[4,128,4,4,128]{4,1,3,2,0:T(8,128)(2,1)} %copy.227, bf16[4,4,52,4,8,128]{5,4,3,2,1,0:T(8,128)(2,1)} %get-tuple-element.32), kind=kOutput, calls=%fused_computation.69 | convolution fusion | flops 873267200 | bytes 10616832 | tf_op jit(solution)/shard_map/kgbpr,bpkgd->brkd/dot_general | solution.py:76
  223.5 6.1 %fusion.65 = bf16[4,416,4,128]{3,1,2,0:T(8,128)(2,1)} fusion(bf16[4,128,4,4,128]{4,1,3,2,0:T(8,128)(2,1)S(1)} %copy-done.17, bf16[4,4,52,4,8,128]{5,4,3,2,1,0:T(8,128)(2,1)} %get-tuple-element.33), kind=kOutput, calls=%fused_computation.70 | convolution fusion | flops 873267200 | bytes 10616832 | tf_op jit(solution)/shard_map/kgbpr,bpkgd->brkd/dot_general | solution.py:76
  238.0 4.4 %all-to-all-start.6 = ((bf16[4,416,512]{2,1,0:T(8,128)(2,1)}), bf16[4,416,512]{2,1,0:T(8,128)(2,1)}, u32[]{:S(2)}, u32[]{:S(2)}) async-start(bf16[4,416,512]{2,1,0:T(8,128)(2,1)} %copy.235), calls=%async_computation.6 | async-start | bytes 3407872 | tf_op jit(solution)/shard_map/all_to_all | solution.py:265
  242.5 28.4 %all-reduce.2.cloned.1.call-done = bf16[512,4,4,128]{0,3,2,1:T(8,128)(2,1)} async-done(((bf16[512,4,4,128]{0,3,2,1:T(8,128)(2,1)}), bf16[512,4,4,128]{0,3,2,1:T(8,128)(2,1)}) %all-reduce.2.cloned.1.call-update) | async-done | bytes 2097168 | tf_op jit(solution)/shard_map/psum | solution.py:221
  270.9 4.5 %multiply_reduce_fusion = (f32[512,4,4]{0,2,1:T(4,128)S(1)}, f32[512,4,4,128]{0,3,2,1:T(8,128)}) fusion(bf16[512,4,4,128]{0,3,2,1:T(8,128)(2,1)S(1)} %copy-done.8, f32[512,4,4]{0,2,1:T(4,128)S(1)} %get-tuple-element.35, bf16[512,4,4,128]{0,3,2,1:T(8,128)(2,1)} %all-reduce.2.cloned.1.call-done), kind=kLoop, calls=%fused_computation.37 | loop fusion | flops 5234688 | bytes 8454144 | tf_op jit(solution)/shard_map/reduce_sum | solution.py:228
  275.4 7.5 %fusion.1 = bf16[4,4,512,416]{2,3,1,0:T(8,128)(2,1)S(1)} fusion(bf16[512,4,4,128]{0,3,2,1:T(8,128)(2,1)S(1)} %copy-done.8, f32[4,4,512]{2,1,0:T(4,128)S(1)} %bitcast.273, f32[4,4,512]{2,1,0:T(4,128)S(1)} %get-tuple-element.34, f32[4,416,512,4]{2,1,3,0:T(8,128)} %get-tuple-element.41, pred[512,416]{0,1:T(8,128)(4,1)S(1)} %get-tuple-element.37, ...), kind=kOutput, calls=%fused_computation.2 | convolution fusion | flops 892862464 | bytes 23248896 | tf_op jit(solution)/shard_map/pkgd,rkd->kgpr/dot_general | solution.py:54
  293.5 7.3 %fusion.3 = bf16[4,4,512,416]{2,3,1,0:T(8,128)(2,1)S(1)} fusion(bf16[512,4,4,128]{0,3,2,1:T(8,128)(2,1)S(1)} %copy-done.8, f32[4,4,512]{2,1,0:T(4,128)S(1)} %bitcast.274, f32[4,4,512]{2,1,0:T(4,128)S(1)} %get-tuple-element.34, f32[4,416,512,4]{2,1,3,0:T(8,128)} %get-tuple-element.39, pred[512,416]{0,1:T(8,128)(4,1)S(1)} %get-tuple-element.36, ...), kind=kOutput, calls=%fused_computation.5 | convolution fusion | flops 892862464 | bytes 23248896 | tf_op jit(solution)/shard_map/pkgd,rkd->kgpr/dot_general | solution.py:54
  307.3 4.3 %fusion.86 = f32[4,128,4,512]{3,1,2,0:T(8,128)S(1)} fusion(bf16[4,4,512,416]{2,3,1,0:T(8,128)(2,1)} %copy-done.10, bf16[416,4,128,1]{2,1,0,3:T(4,128)(2,1)S(1)} %bitcast.271), kind=kOutput, calls=%fused_computation.105 | convolution fusion | flops 872415232 | bytes 11436032 | tf_op jit(solution)/shard_map/kgpr,rkd->pkgd/dot_general | solution.py:60
  311.6 4.4 %multiply_convert_fusion = bf16[4,128,4,512]{3,1,2,0:T(8,128)(2,1)S(1)} fusion(f32[4,128,4,512]{3,1,2,0:T(8,128)S(1)} %fusion.86, bf16[4,4,512,416]{2,3,1,0:T(8,128)(2,1)} %copy-done.9, bf16[416,4,128,1]{2,1,0,3:T(4,128)(2,1)S(1)} %bitcast.269), kind=kOutput, calls=%fused_computation.36 | convolution fusion | flops 875560960 | bytes 13533184 | tf_op jit(solution)/shard_map/kgpr,rkd->pkgd/dot_general | solution.py:60
  318.6 4.0 convolution_convert_fusion.1
  327.6 3.9 copy.236
  331.6 17.5 %all-to-all-done.4 = bf16[4,416,512]{2,1,0:T(8,128)(2,1)S(1)} async-done(((bf16[4,416,512]{2,1,0:T(8,128)(2,1)}), bf16[4,416,512]{2,1,0:T(8,128)(2,1)S(1)}, u32[]{:S(2)}, u32[]{:S(2)}) %all-to-all-start.4) | async-done | bytes 1703968 | tf_op jit(solution)/shard_map/all_to_all | solution.py:258
  353.9 4.0 copy.220
  357.9 16.7 %all-to-all-done.7 = bf16[4,416,512]{2,0,1:T(4,128)(2,1)S(1)} async-done(((bf16[4,416,512]{2,0,1:T(4,128)(2,1)}), bf16[4,416,512]{2,0,1:T(4,128)(2,1)S(1)}, u32[]{:S(2)}, u32[]{:S(2)}) %all-to-all-start.7) | async-done | bytes 1703968 | tf_op jit(solution)/shard_map/all_to_all | solution.py:264
  381.9 5.2 %copy.357 = bf16[4,2,208,512]{3,1,0,2:T(2,128)(2,1)} copy(bf16[4,2,208,512]{3,0,2,1:T(4,128)(2,1)} %bitcast.254) | data formatting | bytes 3407872 | tf_op jit(solution)/shard_map/all_to_all | solution.py:264
  387.1 5.7 %all_to_all.83 = bf16[4,208,1024]{2,0,1:T(4,128)(2,1)} reshape(bf16[4,208,2,512]{3,2,0,1:T(2,128)(2,1)} %bitcast.256) | data formatting | bytes 3407872 | tf_op jit(solution)/shard_map/all_to_all | solution.py:264
  402.3 5.1 %all_to_all.78 = bf16[4,208,1024]{2,1,0:T(8,128)(2,1)} reshape(bf16[4,208,2,512]{3,2,1,0:T(2,128)(2,1)} %bitcast.257) | data formatting | bytes 3407872 | tf_op jit(solution)/shard_map/all_to_all | solution.py:257
  (180 shorter events, 129.0 us)
Async XLA Ops:
  7.2 18.6 %copy-start = (bf16[2,208,1024]{2,1,0:T(8,128)(2,1)S(1)}, bf16[2,208,1024]{2,1,0:T(8,128)(2,1)}, u32[]{:S(2)}) copy-start(bf16[2,208,1024]{2,1,0:T(8,128)(2,1)} %param.12) | copy-start | bytes 2555908
  9.8 5.2 %copy-start.35 = (f32[128]{0:T(128)S(1)}, f32[128]{0:T(128)}, u32[]{:S(2)}) copy-start(f32[128]{0:T(128)} %param.14) | copy-start | bytes 1540
  9.8 5.2 %copy-start.37 = (s32[4,2]{0,1:T(2,128)S(1)}, s32[4,2]{0,1:T(2,128)}, u32[]{:S(2)}) copy-start(s32[4,2]{0,1:T(2,128)} %param.17) | copy-start | bytes 100
  9.8 5.2 %copy-start.16 = (bf16[2,208,1024]{2,1,0:T(8,128)(2,1)S(1)}, bf16[2,208,1024]{2,1,0:T(8,128)(2,1)}, u32[]{:S(2)}) copy-start(bf16[2,208,1024]{2,1,0:T(8,128)(2,1)} %param.11) | copy-start | bytes 2555908
  16.8 6.2 %copy-start.26 = (bf16[1,128,2048]{2,1,0:T(8,128)(2,1)S(1)}, bf16[1,128,2048]{2,1,0:T(8,128)(2,1)}, u32[]{:S(2)}) copy-start(bf16[1,128,2048]{2,1,0:T(8,128)(2,1)} %param.10) | copy-start | bytes 1572868
  18.6 26.6 %all-to-all-start.2 = ((bf16[4,208,1024]{2,1,0:T(8,128)(2,1)}), bf16[4,208,1024]{2,1,0:T(8,128)(2,1)}, u32[]{:S(2)}, u32[]{:S(2)}) async-start(bf16[4,208,1024]{2,1,0:T(8,128)(2,1)} %copy.195), calls=%async_computation.2 | async-start | bytes 3407872 | tf_op jit(solution)/shard_map/all_to_all | solution.py:182
  23.0 117.4 %all-gather.3.cloned.1.call-start = ((), (), s32[]{:S(2)}) async-start(), calls=%async_computation.9 | async-start | bytes 2621440 | tf_op jit(solution)/shard_map/all_gather | solution.py:213
  23.4 3.9 copy-start.5
  45.1 25.0 %all-to-all-start = ((bf16[4,208,1024]{2,1,0:T(8,128)(2,1)}), bf16[4,208,1024]{2,1,0:T(8,128)(2,1)S(1)}, u32[]{:S(2)}, u32[]{:S(2)}) async-start(bf16[4,208,1024]{2,1,0:T(8,128)(2,1)} %copy.189), calls=%async_computation | async-start | bytes 3407872 | tf_op jit(solution)/shard_map/all_to_all | solution.py:189
  48.7 27.1 %copy-start.27 = (bf16[1,128,2048]{2,1,0:T(8,128)(2,1)S(1)}, bf16[1,128,2048]{2,1,0:T(8,128)(2,1)}, u32[]{:S(2)}) copy-start(bf16[1,128,2048]{2,1,0:T(8,128)(2,1)} %param.19) | copy-start | bytes 1572868
  53.0 24.2 %copy-start.41 = (s32[4]{0:T(128)S(1)}, s32[4]{0:T(128)}, u32[]{:S(2)}) copy-start(s32[4]{0:T(128)} %param.16) | copy-start | bytes 52
  71.4 29.2 %all-to-all-start.3 = ((bf16[4,208,1024]{1,0,2:T(4,128)(2,1)}), bf16[4,208,1024]{1,0,2:T(4,128)(2,1)S(1)}, u32[]{:S(2)}, u32[]{:S(2)}) async-start(bf16[4,208,1024]{1,0,2:T(4,128)(2,1)} %copy.196), calls=%async_computation.3 | async-start | bytes 4194304 | tf_op jit(solution)/shard_map/all_to_all | solution.py:181
  75.1 128.2 %all-gather.5.cloned.1.call-start = ((), (), s32[]{:S(2)}) async-start(), calls=%async_computation.11 | async-start | bytes 2621440 | tf_op jit(solution)/shard_map/all_gather | solution.py:214
  100.6 29.3 %all-to-all-start.1 = ((bf16[4,208,1024]{1,0,2:T(4,128)(2,1)}), bf16[4,208,1024]{1,0,2:T(4,128)(2,1)}, u32[]{:S(2)}, u32[]{:S(2)}) async-start(bf16[4,208,1024]{1,0,2:T(4,128)(2,1)} %copy.190), calls=%async_computation.1 | async-start | bytes 4194304 | tf_op jit(solution)/shard_map/all_to_all | solution.py:188
  105.4 165.5 %all-reduce.2.cloned.1.call-start = ((), (), s32[]{:S(2)}) async-start(), calls=%async_computation.10 | async-start | bytes 4194304 | tf_op jit(solution)/shard_map/psum | solution.py:221
  136.4 3.9 copy-start.20
  140.4 8.4 %copy-start.22 = (bf16[416,4,128]{2,1,0:T(4,128)(2,1)S(1)}, bf16[416,4,128]{2,1,0:T(4,128)(2,1)}, u32[]{:S(2)}) copy-start(bf16[416,4,128]{2,1,0:T(4,128)(2,1)} %reshape_squeeze.17) | copy-start | bytes 1277956
  140.4 8.4 %copy-start.38 = (bf16[512,4,4,128]{3,0,2,1:T(8,128)(2,1)S(1)}, bf16[512,4,4,128]{3,0,2,1:T(8,128)(2,1)}, u32[]{:S(2)}) copy-start(bf16[512,4,4,128]{3,0,2,1:T(8,128)(2,1)} %all-gather.3.cloned.1.call-done) | copy-start | bytes 6291460
  175.0 8.8 %copy-start.2 = (f32[4,416,512,4]{2,1,3,0:T(8,128)S(1)}, f32[4,416,512,4]{2,1,3,0:T(8,128)}, u32[]{:S(2)}) copy-start(f32[4,416,512,4]{2,1,3,0:T(8,128)} %get-tuple-element.39) | copy-start | bytes 40894468
  215.2 8.3 %copy-start.17 = (bf16[4,128,4,4,128]{4,1,3,2,0:T(8,128)(2,1)S(1)}, bf16[4,128,4,4,128]{4,1,3,2,0:T(8,128)(2,1)}, u32[]{:S(2)}) copy-start(bf16[4,128,4,4,128]{4,1,3,2,0:T(8,128)(2,1)} %copy.227) | copy-start | bytes 6291460
  236.5 34.4 %copy-start.8 = (bf16[512,4,4,128]{0,3,2,1:T(8,128)(2,1)S(1)}, bf16[512,4,4,128]{0,3,2,1:T(8,128)(2,1)}, u32[]{:S(2)}) copy-start(bf16[512,4,4,128]{0,3,2,1:T(8,128)(2,1)} %all-gather.5.cloned.1.call-done) | copy-start | bytes 6291460
  238.0 86.1 %all-to-all-start.6 = ((bf16[4,416,512]{2,1,0:T(8,128)(2,1)}), bf16[4,416,512]{2,1,0:T(8,128)(2,1)}, u32[]{:S(2)}, u32[]{:S(2)}) async-start(bf16[4,416,512]{2,1,0:T(8,128)(2,1)} %copy.235), calls=%async_computation.6 | async-start | bytes 3407872 | tf_op jit(solution)/shard_map/all_to_all | solution.py:265
  242.4 174.0 %reduce-scatter.4.cloned.1.call-start = ((), (), s32[]{:S(2)}) async-start(), calls=%async_computation.12 | async-start | bytes 2621440
  275.4 10.2 %copy-start.39 = (bf16[512,4,4,128]{3,0,2,1:T(8,128)(2,1)S(1)}, bf16[512,4,4,128]{3,0,2,1:T(8,128)(2,1)}, u32[]{:S(2)}) copy-start(bf16[512,4,4,128]{3,0,2,1:T(8,128)(2,1)} %all-gather.3.cloned.1.call-done) | copy-start | bytes 6291460
  293.5 10.2 %copy-start.40 = (bf16[512,4,4,128]{3,0,2,1:T(8,128)(2,1)S(1)}, bf16[512,4,4,128]{3,0,2,1:T(8,128)(2,1)}, u32[]{:S(2)}) copy-start(bf16[512,4,4,128]{3,0,2,1:T(8,128)(2,1)} %all-gather.3.cloned.1.call-done) | copy-start | bytes 6291460
  307.3 4.3 %copy-start.21 = (bf16[416,4,128]{2,1,0:T(4,128)(2,1)S(1)}, bf16[416,4,128]{2,1,0:T(4,128)(2,1)}, u32[]{:S(2)}) copy-start(bf16[416,4,128]{2,1,0:T(4,128)(2,1)} %reshape_squeeze.19) | copy-start | bytes 1277956
  324.0 25.0 %all-to-all-start.4 = ((bf16[4,416,512]{2,1,0:T(8,128)(2,1)}), bf16[4,416,512]{2,1,0:T(8,128)(2,1)S(1)}, u32[]{:S(2)}, u32[]{:S(2)}) async-start(bf16[4,416,512]{2,1,0:T(8,128)(2,1)} %copy.219), calls=%async_computation.4 | async-start | bytes 3407872 | tf_op jit(solution)/shard_map/all_to_all | solution.py:258
  350.2 24.4 %all-to-all-start.7 = ((bf16[4,416,512]{2,0,1:T(4,128)(2,1)}), bf16[4,416,512]{2,0,1:T(4,128)(2,1)S(1)}, u32[]{:S(2)}, u32[]{:S(2)}) async-start(bf16[4,416,512]{2,0,1:T(4,128)(2,1)} %copy.236), calls=%async_computation.7 | async-start | bytes 3407872 | tf_op jit(solution)/shard_map/all_to_all | solution.py:264
  375.8 23.5 %all-to-all-start.5 = ((bf16[4,416,512]{2,0,1:T(4,128)(2,1)}), bf16[4,416,512]{2,0,1:T(4,128)(2,1)S(1)}, u32[]{:S(2)}, u32[]{:S(2)}) async-start(bf16[4,416,512]{2,0,1:T(4,128)(2,1)} %copy.220), calls=%async_computation.5 | async-start | bytes 3407872 | tf_op jit(solution)/shard_map/all_to_all | solution.py:257
  407.4 4.7 %copy-start.4 = (f32[52,8,8,128]{3,2,1,0:T(8,128)S(1)}, f32[52,8,8,128]{3,2,1,0:T(8,128)}, u32[]{:S(2)}) copy-start(f32[52,8,8,128]{3,2,1,0:T(8,128)} %copy-done.3) | copy-start | bytes 5111812
  407.4 4.7 %copy-start.36 = (f32[128]{0:T(128)S(1)}, f32[128]{0:T(128)}, u32[]{:S(2)}) copy-start(f32[128]{0:T(128)} %param.14) | copy-start | bytes 1540
  409.5 3.4 copy-start.19
  (22 other events, 46.5 us)
Sparse Core Ops, SparseCore 0:
  25.9 48.7 all-gather.2
  78.1 47.8 all-gather.4
  187.8 82.9 all-reduce.1
  318.7 42.6 reduce-scatter.3
where the time goes:
time: 434 us; the launch traced here: 427 us
  waiting for transfers between devices  128 us (29%)
  local copies, waits for them, and re-layouts  109 us (25%)
  matrix products  85 us (20%)
  other arithmetic  36.4 us (8%)
  starting transfers between devices  32.3 us (7%)
  blocking collectives  19.6 us (5%)
  between operations  15.7 us (4%)
    psum x1, waiting for transfers between devices, shards(): lax.psum(part_weighted.astype(jnp.bfloat16), 'seq').astype(jnp.float32)  28.4 us
    unnamed x92, local copies, waits for them, and re-layouts  26.6 us
    psum x1, blocking collectives, shards(): lax.psum(part_sum.astype(jnp.bfloat16), 'seq').astype(jnp.float32)  19.6 us
    all_to_all x1, waiting for transfers between devices, shards(): lax.all_to_all(back_keys, 'conv', split_axis=0, concat_axis=0, tiled=True)  17.5 us
    all_to_all x1, waiting for transfers between devices, shards(): lax.all_to_all(lax.all_to_all(outgoing_keys, 'conv', split_axis=0, concat...  17.2 us
    all_to_all x1, waiting for transfers between devices, shards(): lax.all_to_all(send_values, 'conv', split_axis=0, concat_axis=0, tiled=True)  17.2 us
    all_to_all x1, waiting for transfers between devices, shards(): lax.all_to_all(lax.all_to_all(back_values, 'conv', split_axis=0, concat_a...  16.7 us
    all_to_all x1, waiting for transfers between devices, shards(): lax.all_to_all(outgoing_keys, 'conv', split_axis=0, concat_axis=0, tiled=...  16.1 us
  transfers between devices with their start and end apart: 12, of which 8 were waited for; matrix products, arithmetic and copies ran while one was open for 45% of the time, Pallas kernels for 0%

commit v1 on v0

--- a/solution.py
+++ b/solution.py
@@ -218,7 +218,9 @@
         all_queries, tile_keys, tile_values, seen_all, row_start, score_scale
     )
     all_weighted, all_weight_sum = (
-        lax.psum(part_weighted.astype(jnp.bfloat16), "seq").astype(jnp.float32),
+        jnp.sum(lax.all_gather(part_weighted.astype(jnp.bfloat16), "seq"), axis=0).astype(
+            jnp.float32
+        ),
         lax.psum(part_sum.astype(jnp.bfloat16), "seq").astype(jnp.float32),
     )
     safe_all = jnp.where(all_weight_sum > 0, all_weight_sum, 1.0)

time: 434 us -> 512 us (1.18)
  waiting for transfers between devices: 128 us -> 179 us
  other arithmetic: 36.4 us -> 49.4 us
  local copies, waits for them, and re-layouts: 109 us -> 120 us
    all_gather x0 -> x1, waiting for transfers between devices: none -> 80 us  [shards(): lax.all_gather(part_weighted.astype(jnp.bfloat16), 'seq')]
    psum x1 -> x0, waiting for transfers between devices: 28.4 us -> none  [shards(): lax.psum(part_weighted.astype(jnp.bfloat16), 'seq').astype(jnp.float32)]
    all_gather x0 -> x1, local copies, waits for them, and re-layouts: none -> 14.6 us  [shards(): lax.all_gather(part_weighted.astype(jnp.bfloat16), 'seq')]
    reduce_sum x0 -> x1, other arithmetic: none -> 13 us  [shards(): jnp.sum(lax.all_gather(part_weighted.astype(jnp.bfloat16), 'seq'), axis=0)]
    reshape x2 -> x0, local copies, waits for them, and re-layouts: 5.14 us -> none  [tile_gradients(): grad_bf.reshape(block_count, block_tokens, kv_local, group_size, head_size)]
    unnamed x92 -> x101, local copies, waits for them, and re-layouts: 26.6 us -> 24.6 us
  transfers between devices with their start and end apart: 12 -> 12, of which waited for: 8 -> 8; matrix products, arithmetic and copies ran while one was open for 45% -> 44% of each run, Pallas kernels for 0% -> 0%
where the time goes in v1:
time: 512 us; the launch traced here: 504 us
  waiting for transfers between devices  179 us (35%)
  local copies, waits for them, and re-layouts  120 us (23%)
  matrix products  86.8 us (17%)
  other arithmetic  49.4 us (10%)
  starting transfers between devices  32.3 us (6%)
  blocking collectives  20.3 us (4%)
  between operations  15.8 us (3%)
    all_gather x1, waiting for transfers between devices, shards(): lax.all_gather(part_weighted.astype(jnp.bfloat16), 'seq')  80 us
    unnamed x101, local copies, waits for them, and re-layouts  24.6 us
    psum x1, blocking collectives, shards(): lax.psum(part_sum.astype(jnp.bfloat16), 'seq').astype(jnp.float32)  20.3 us
    all_to_all x1, waiting for transfers between devices, shards(): lax.all_to_all(back_keys, 'conv', split_axis=0, concat_axis=0, tiled=True)  17.5 us
    all_to_all x1, waiting for transfers between devices, shards(): lax.all_to_all(send_values, 'conv', split_axis=0, concat_axis=0, tiled=True)  17.2 us
    all_to_all x1, waiting for transfers between devices, shards(): lax.all_to_all(lax.all_to_all(outgoing_keys, 'conv', split_axis=0, concat...  17 us
    all_to_all x1, waiting for transfers between devices, shards(): lax.all_to_all(lax.all_to_all(back_values, 'conv', split_axis=0, concat_a...  16.7 us
    all_to_all x1, waiting for transfers between devices, shards(): lax.all_to_all(outgoing_keys, 'conv', split_axis=0, concat_axis=0, tiled=...  16.2 us
  transfers between devices with their start and end apart: 12, of which 8 were waited for; matrix products, arithmetic and copies ran while one was open for 44% of the time, Pallas kernels for 0%

profile of v1, /device:TPU:0, one launch (start us, length us, event | category | flops | bytes accessed | tf_op | source)
XLA Modules:
  0.0 503.9 jit_solution(2944736521895584661)
XLA Ops:
  18.6 4.4 all-to-all-start.2
  29.0 16.2 %all-to-all-done.2 = bf16[4,208,1024]{2,1,0:T(8,128)(2,1)} async-done(((bf16[4,208,1024]{2,1,0:T(8,128)(2,1)}), bf16[4,208,1024]{2,1,0:T(8,128)(2,1)}, u32[]{:S(2)}, u32[]{:S(2)}) %all-to-all-start.2) | async-done | bytes 1703968 | tf_op jit(solution)/shard_map/all_to_all | solution.py:182
  48.8 4.2 copy.194
  53.0 17.2 %all-to-all-done = bf16[4,208,1024]{2,1,0:T(8,128)(2,1)S(1)} async-done(((bf16[4,208,1024]{2,1,0:T(8,128)(2,1)}), bf16[4,208,1024]{2,1,0:T(8,128)(2,1)S(1)}, u32[]{:S(2)}, u32[]{:S(2)}) %all-to-all-start) | async-done | bytes 1703968 | tf_op jit(solution)/shard_map/all_to_all | solution.py:189
  79.5 4.2 copy.188
  83.6 17.0 %all-to-all-done.3 = bf16[4,208,1024]{1,0,2:T(4,128)(2,1)S(1)} async-done(((bf16[4,208,1024]{1,0,2:T(4,128)(2,1)}), bf16[4,208,1024]{1,0,2:T(4,128)(2,1)S(1)}, u32[]{:S(2)}, u32[]{:S(2)}) %all-to-all-start.3) | async-done | bytes 1703968 | tf_op jit(solution)/shard_map/all_to_all | solution.py:181
  100.6 4.8 all-to-all-start.1
  106.0 4.0 copy.195
  117.9 12.0 %all-to-all-done.1 = bf16[4,208,1024]{1,0,2:T(4,128)(2,1)} async-done(((bf16[4,208,1024]{1,0,2:T(4,128)(2,1)}), bf16[4,208,1024]{1,0,2:T(4,128)(2,1)}, u32[]{:S(2)}, u32[]{:S(2)}) %all-to-all-start.1) | async-done | bytes 1703968 | tf_op jit(solution)/shard_map/all_to_all | solution.py:188
  130.0 5.4 %copy.189 = bf16[4,208,2,512]{3,0,1,2:T(4,128)(2,1)S(1)} copy(bf16[4,208,2,512]{1,0,3,2:T(4,128)(2,1)} %bitcast.2) | data formatting | bytes 3407872 | tf_op jit(solution)/shard_map/all_to_all | solution.py:188
  140.4 8.7 %fusion.8 = (f32[4,4,512]{2,1,0:T(4,128)S(1)}, f32[4,416,512,4]{2,1,3,0:T(8,128)}) fusion(pred[512,416]{0,1:T(8,128)(4,1)S(1)} %get-tuple-element.37, bf16[512,4,4,128]{3,0,2,1:T(8,128)(2,1)} %all-gather.5.cloned.1.call-done, bf16[416,4,128,1]{2,1,0,3:T(4,128)(2,1)S(1)} %bitcast.269), kind=kOutput, calls=%fused_computation.12 | convolution fusion | flops 882630656 | bytes 16400384 | tf_op jit(solution)/shard_map/pkgd,rkd->kgpr/dot_general | solution.py:24
  152.6 11.1 %fusion.10 = f32[4,128,4,512]{3,1,2,0:T(8,128)S(1)} fusion(f32[4,416,512,4]{2,1,3,0:T(8,128)} %get-tuple-element.41, pred[512,416]{0,1:T(8,128)(4,1)S(1)} %get-tuple-element.37, bf16[416,4,128,1]{2,1,0,3:T(4,128)(2,1)S(1)} %bitcast.261), kind=kOutput, calls=%fused_computation.14 | convolution fusion | flops 882638848 | bytes 18464768 | tf_op jit(solution)/shard_map/kgpr,rkd->pkgd/dot_general | solution.py:32
  167.7 20.3 %psum.7 = bf16[4,4,512]{2,1,0:T(4,128)(2,1)S(1)} all-reduce(bf16[4,4,512]{2,1,0:T(4,128)(2,1)S(1)} %add_convert_fusion.1), channel_id=1, replica_groups=mesh['conv'=4,'seq'=4,'tensor'=2] {'seq'}, use_global_device_ids=true, to_apply=%region_5.6 | all-reduce | flops 8192 | bytes 32768 | tf_op jit(solution)/shard_map/psum | solution.py:224
  188.0 15.4 %convert_bitcast_fusion.1 = (bf16[4,4,52,4,8,128]{5,4,3,2,1,0:T(8,128)(2,1)}, bf16[4,4,52,4,8,128]{5,4,3,2,1,0:T(8,128)(2,1)}) fusion(f32[4,4,512]{2,1,0:T(4,128)S(1)} %get-tuple-element.34, f32[4,416,512,4]{2,1,3,0:T(8,128)} %copy-done.2, pred[512,416]{0,1:T(8,128)(4,1)S(1)} %get-tuple-element.36, f32[4,416,512,4]{2,1,3,0:T(8,128)} %get-tuple-element.41, ...), kind=kLoop, calls=%fused_computation.29 | loop fusion | flops 27262976 | bytes 41353216
  203.4 6.8 %fusion.64 = bf16[4,416,4,128]{3,1,2,0:T(8,128)(2,1)} fusion(bf16[4,128,4,4,128]{4,1,0,3,2:T(8,128)(2,1)} %bitcast.265, bf16[4,4,52,4,8,128]{5,4,3,2,1,0:T(8,128)(2,1)} %get-tuple-element.32), kind=kOutput, calls=%fused_computation.71 | convolution fusion | flops 873267200 | bytes 10616832 | tf_op jit(solution)/shard_map/kgbpr,bpkgd->brkd/dot_general | solution.py:76
  218.4 6.1 %fusion.69 = bf16[4,416,4,128]{3,1,2,0:T(8,128)(2,1)} fusion(bf16[4,128,4,4,128]{4,1,0,3,2:T(8,128)(2,1)S(1)} %bitcast.266, bf16[4,4,52,4,8,128]{5,4,3,2,1,0:T(8,128)(2,1)} %get-tuple-element.33), kind=kOutput, calls=%fused_computation.72 | convolution fusion | flops 873267200 | bytes 10616832 | tf_op jit(solution)/shard_map/kgbpr,bpkgd->brkd/dot_general | solution.py:76
  233.0 4.4 all-to-all-start.6
  237.4 80.0 %all-gather.9.cloned.1.call-done = bf16[2048,4,4,128]{0,3,2,1:T(8,128)(2,1)} async-done(((bf16[512,4,4,128]{0,3,2,1:T(8,128)(2,1)}), bf16[2048,4,4,128]{0,3,2,1:T(8,128)(2,1)}) %all-gather.9.cloned.1.call-update) | async-done | bytes 8388624 | tf_op jit(solution)/shard_map/all_gather | solution.py:221
  317.4 14.6 %reshape.250 = bf16[4,512,4,4,128]{1,0,4,3,2:T(4,128)(2,1)} reshape(bf16[2048,4,4,128]{0,3,2,1:T(8,128)(2,1)} %all-gather.9.cloned.1.call-done) | data formatting | bytes 16777216 | tf_op jit(solution)/shard_map/all_gather | solution.py:221
  332.1 13.0 %reduce_sum.121 = bf16[512,4,4,128]{0,3,2,1:T(8,128)(2,1)} reduce(bf16[4,512,4,4,128]{1,0,4,3,2:T(4,128)(2,1)} %reshape.250, bf16[]{:T(256)} %constant.30.clone.1), dimensions={0}, to_apply=%region_2.3 | reduce | flops 3145728 | bytes 10485762 | tf_op jit(solution)/shard_map/reduce_sum | solution.py:221
  348.1 4.5 multiply_reduce_fusion
  352.6 7.4 %fusion.1 = bf16[4,4,512,416]{2,3,1,0:T(8,128)(2,1)S(1)} fusion(bf16[512,4,4,128]{3,0,2,1:T(8,128)(2,1)S(1)} %copy-done.17, f32[4,4,512]{2,1,0:T(4,128)S(1)} %bitcast.274, f32[4,4,512]{2,1,0:T(4,128)S(1)} %get-tuple-element.34, f32[4,416,512,4]{2,1,3,0:T(8,128)} %get-tuple-element.41, pred[512,416]{0,1:T(8,128)(4,1)S(1)} %get-tuple-element.37, ...), kind=kOutput, calls=%fused_computation.2 | convolution fusion | flops 892862464 | bytes 23248896 | tf_op jit(solution)/shard_map/pkgd,rkd->kgpr/dot_general | solution.py:54
  370.8 7.5 %fusion.3 = bf16[4,4,512,416]{2,3,1,0:T(8,128)(2,1)S(1)} fusion(bf16[512,4,4,128]{3,0,2,1:T(8,128)(2,1)S(1)} %copy-done.18, f32[4,4,512]{2,1,0:T(4,128)S(1)} %bitcast.275, f32[4,4,512]{2,1,0:T(4,128)S(1)} %get-tuple-element.34, f32[4,416,512,4]{2,1,3,0:T(8,128)} %copy-done.2, pred[512,416]{0,1:T(8,128)(4,1)S(1)} %get-tuple-element.36, ...), kind=kOutput, calls=%fused_computation.5 | convolution fusion | flops 892862464 | bytes 23248896 | tf_op jit(solution)/shard_map/pkgd,rkd->kgpr/dot_general | solution.py:54
  384.8 4.3 fusion.92
  389.1 4.4 multiply_convert_fusion
  405.0 3.9 copy.235
  408.9 17.5 %all-to-all-done.4 = bf16[4,416,512]{2,1,0:T(8,128)(2,1)S(1)} async-done(((bf16[4,416,512]{2,1,0:T(8,128)(2,1)}), bf16[4,416,512]{2,1,0:T(8,128)(2,1)S(1)}, u32[]{:S(2)}, u32[]{:S(2)}) %all-to-all-start.4) | async-done | bytes 1703968 | tf_op jit(solution)/shard_map/all_to_all | solution.py:260
  431.3 4.0 copy.219
  435.3 16.7 %all-to-all-done.7 = bf16[4,416,512]{2,0,1:T(4,128)(2,1)S(1)} async-done(((bf16[4,416,512]{2,0,1:T(4,128)(2,1)}), bf16[4,416,512]{2,0,1:T(4,128)(2,1)S(1)}, u32[]{:S(2)}, u32[]{:S(2)}) %all-to-all-start.7) | async-done | bytes 1703968 | tf_op jit(solution)/shard_map/all_to_all | solution.py:266
  456.9 5.3 %copy.362 = bf16[4,2,208,512]{3,1,0,2:T(2,128)(2,1)} copy(bf16[4,2,208,512]{3,0,2,1:T(4,128)(2,1)} %bitcast.253) | data formatting | bytes 3407872 | tf_op jit(solution)/shard_map/all_to_all | solution.py:266
  462.1 5.7 %all_to_all.83 = bf16[4,208,1024]{2,0,1:T(4,128)(2,1)} reshape(bf16[4,208,2,512]{3,2,0,1:T(2,128)(2,1)} %bitcast.255) | data formatting | bytes 3407872 | tf_op jit(solution)/shard_map/all_to_all | solution.py:266
  479.6 5.1 %all_to_all.78 = bf16[4,208,1024]{2,1,0:T(8,128)(2,1)} reshape(bf16[4,208,2,512]{3,2,1,0:T(2,128)(2,1)} %bitcast.256) | data formatting | bytes 3407872 | tf_op jit(solution)/shard_map/all_to_all | solution.py:259
  (191 shorter events, 132.1 us)
Async XLA Ops:
  7.2 18.6 %copy-start = (bf16[2,208,1024]{2,1,0:T(8,128)(2,1)S(1)}, bf16[2,208,1024]{2,1,0:T(8,128)(2,1)}, u32[]{:S(2)}) copy-start(bf16[2,208,1024]{2,1,0:T(8,128)(2,1)} %param.12) | copy-start | bytes 2555908
  9.8 5.2 %copy-start.37 = (f32[128]{0:T(128)S(1)}, f32[128]{0:T(128)}, u32[]{:S(2)}) copy-start(f32[128]{0:T(128)} %param.14) | copy-start | bytes 1540
  9.8 5.2 %copy-start.39 = (s32[4,2]{0,1:T(2,128)S(1)}, s32[4,2]{0,1:T(2,128)}, u32[]{:S(2)}) copy-start(s32[4,2]{0,1:T(2,128)} %param.17) | copy-start | bytes 100
  9.9 5.2 %copy-start.15 = (bf16[2,208,1024]{2,1,0:T(8,128)(2,1)S(1)}, bf16[2,208,1024]{2,1,0:T(8,128)(2,1)}, u32[]{:S(2)}) copy-start(bf16[2,208,1024]{2,1,0:T(8,128)(2,1)} %param.11) | copy-start | bytes 2555908
  15.1 10.7 %copy-start.40 = (pred[4,2]{0,1:T(4,128)(4,1)}, pred[4,2]{0,1:T(4,128)(4,1)S(1)}, u32[]{:S(2)}) copy-start(pred[4,2]{0,1:T(4,128)(4,1)S(1)} %broadcast_compare_fusion) | copy-start | bytes 28
  16.9 6.2 %copy-start.27 = (bf16[1,128,2048]{2,1,0:T(8,128)(2,1)S(1)}, bf16[1,128,2048]{2,1,0:T(8,128)(2,1)}, u32[]{:S(2)}) copy-start(bf16[1,128,2048]{2,1,0:T(8,128)(2,1)} %param.10) | copy-start | bytes 1572868
  18.6 26.6 %all-to-all-start.2 = ((bf16[4,208,1024]{2,1,0:T(8,128)(2,1)}), bf16[4,208,1024]{2,1,0:T(8,128)(2,1)}, u32[]{:S(2)}, u32[]{:S(2)}) async-start(bf16[4,208,1024]{2,1,0:T(8,128)(2,1)} %copy.193), calls=%async_computation.2 | async-start | bytes 3407872 | tf_op jit(solution)/shard_map/all_to_all | solution.py:182
  23.0 117.4 %all-gather.5.cloned.1.call-start = ((), (), s32[]{:S(2)}) async-start(), calls=%async_computation.9 | async-start | bytes 2621440 | tf_op jit(solution)/shard_map/all_gather | solution.py:213
  45.2 25.0 %all-to-all-start = ((bf16[4,208,1024]{2,1,0:T(8,128)(2,1)}), bf16[4,208,1024]{2,1,0:T(8,128)(2,1)S(1)}, u32[]{:S(2)}, u32[]{:S(2)}) async-start(bf16[4,208,1024]{2,1,0:T(8,128)(2,1)} %copy.187), calls=%async_computation | async-start | bytes 3407872 | tf_op jit(solution)/shard_map/all_to_all | solution.py:189
  48.7 27.1 %copy-start.28 = (bf16[1,128,2048]{2,1,0:T(8,128)(2,1)S(1)}, bf16[1,128,2048]{2,1,0:T(8,128)(2,1)}, u32[]{:S(2)}) copy-start(bf16[1,128,2048]{2,1,0:T(8,128)(2,1)} %param.19) | copy-start | bytes 1572868
  53.0 24.5 %copy-start.45 = (s32[4]{0:T(128)S(1)}, s32[4]{0:T(128)}, u32[]{:S(2)}) copy-start(s32[4]{0:T(128)} %param.16) | copy-start | bytes 52
  71.4 29.2 %all-to-all-start.3 = ((bf16[4,208,1024]{1,0,2:T(4,128)(2,1)}), bf16[4,208,1024]{1,0,2:T(4,128)(2,1)S(1)}, u32[]{:S(2)}, u32[]{:S(2)}) async-start(bf16[4,208,1024]{1,0,2:T(4,128)(2,1)} %copy.194), calls=%async_computation.3 | async-start | bytes 4194304 | tf_op jit(solution)/shard_map/all_to_all | solution.py:181
  75.2 128.2 %all-gather.7.cloned.1.call-start = ((), (), s32[]{:S(2)}) async-start(), calls=%async_computation.10 | async-start | bytes 2621440 | tf_op jit(solution)/shard_map/all_gather | solution.py:214
  100.6 29.4 %all-to-all-start.1 = ((bf16[4,208,1024]{1,0,2:T(4,128)(2,1)}), bf16[4,208,1024]{1,0,2:T(4,128)(2,1)}, u32[]{:S(2)}, u32[]{:S(2)}) async-start(bf16[4,208,1024]{1,0,2:T(4,128)(2,1)} %copy.188), calls=%async_computation.1 | async-start | bytes 4194304 | tf_op jit(solution)/shard_map/all_to_all | solution.py:188
  105.4 212.0 %all-gather.9.cloned.1.call-start = ((), (), s32[]{:S(2)}) async-start(), calls=%async_computation.11 | async-start | bytes 10485760 | tf_op jit(solution)/shard_map/all_gather | solution.py:221
  140.4 8.7 %copy-start.23 = (bf16[416,4,128]{2,1,0:T(4,128)(2,1)S(1)}, bf16[416,4,128]{2,1,0:T(4,128)(2,1)}, u32[]{:S(2)}) copy-start(bf16[416,4,128]{2,1,0:T(4,128)(2,1)} %reshape_squeeze.17) | copy-start | bytes 1277956
  140.4 8.7 %copy-start.42 = (bf16[512,4,4,128]{3,0,2,1:T(8,128)(2,1)S(1)}, bf16[512,4,4,128]{3,0,2,1:T(8,128)(2,1)}, u32[]{:S(2)}) copy-start(bf16[512,4,4,128]{3,0,2,1:T(8,128)(2,1)} %all-gather.5.cloned.1.call-done) | copy-start | bytes 6291460
  152.6 11.2 %copy-start.2 = (f32[4,416,512,4]{2,1,3,0:T(8,128)}, f32[4,416,512,4]{2,1,3,0:T(8,128)S(1)}, u32[]{:S(2)}) copy-start(f32[4,416,512,4]{2,1,3,0:T(8,128)S(1)} %get-tuple-element.39) | copy-start | bytes 40894468
  210.1 8.3 %copy-start.16 = (bf16[512,4,4,128]{3,0,2,1:T(8,128)(2,1)S(1)}, bf16[512,4,4,128]{3,0,2,1:T(8,128)(2,1)}, u32[]{:S(2)}) copy-start(bf16[512,4,4,128]{3,0,2,1:T(8,128)(2,1)} %all-gather.7.cloned.1.call-done) | copy-start | bytes 6291460
  233.0 168.4 %all-to-all-start.6 = ((bf16[4,416,512]{2,1,0:T(8,128)(2,1)}), bf16[4,416,512]{2,1,0:T(8,128)(2,1)}, u32[]{:S(2)}, u32[]{:S(2)}) async-start(bf16[4,416,512]{2,1,0:T(8,128)(2,1)} %copy.234), calls=%async_computation.6 | async-start | bytes 3407872 | tf_op jit(solution)/shard_map/all_to_all | solution.py:267
  237.4 256.4 %reduce-scatter.4.cloned.1.call-start = ((), (), s32[]{:S(2)}) async-start(), calls=%async_computation.12 | async-start | bytes 2621440
  348.1 4.5 copy-start.17
  352.6 10.1 %copy-start.43 = (bf16[512,4,4,128]{3,0,2,1:T(8,128)(2,1)S(1)}, bf16[512,4,4,128]{3,0,2,1:T(8,128)(2,1)}, u32[]{:S(2)}) copy-start(bf16[512,4,4,128]{3,0,2,1:T(8,128)(2,1)} %all-gather.5.cloned.1.call-done) | copy-start | bytes 6291460
  365.9 5.0 copy-start.18
  370.8 10.4 %copy-start.44 = (bf16[512,4,4,128]{3,0,2,1:T(8,128)(2,1)S(1)}, bf16[512,4,4,128]{3,0,2,1:T(8,128)(2,1)}, u32[]{:S(2)}) copy-start(bf16[512,4,4,128]{3,0,2,1:T(8,128)(2,1)} %all-gather.5.cloned.1.call-done) | copy-start | bytes 6291460
  401.4 25.0 %all-to-all-start.4 = ((bf16[4,416,512]{2,1,0:T(8,128)(2,1)}), bf16[4,416,512]{2,1,0:T(8,128)(2,1)S(1)}, u32[]{:S(2)}, u32[]{:S(2)}) async-start(bf16[4,416,512]{2,1,0:T(8,128)(2,1)} %copy.218), calls=%async_computation.4 | async-start | bytes 3407872 | tf_op jit(solution)/shard_map/all_to_all | solution.py:260
  427.6 24.4 %all-to-all-start.7 = ((bf16[4,416,512]{2,0,1:T(4,128)(2,1)}), bf16[4,416,512]{2,0,1:T(4,128)(2,1)S(1)}, u32[]{:S(2)}, u32[]{:S(2)}) async-start(bf16[4,416,512]{2,0,1:T(4,128)(2,1)} %copy.235), calls=%async_computation.7 | async-start | bytes 3407872 | tf_op jit(solution)/shard_map/all_to_all | solution.py:266
  431.3 25.6 %copy-start.36 = (f32[128]{0:T(128)S(1)}, f32[128]{0:T(128)}, u32[]{:S(2)}) copy-start(f32[128]{0:T(128)} %param.13) | copy-start | bytes 1540
  453.1 23.5 %all-to-all-start.5 = ((bf16[4,416,512]{2,0,1:T(4,128)(2,1)}), bf16[4,416,512]{2,0,1:T(4,128)(2,1)S(1)}, u32[]{:S(2)}, u32[]{:S(2)}) async-start(bf16[4,416,512]{2,0,1:T(4,128)(2,1)} %copy.219), calls=%async_computation.5 | async-start | bytes 3407872 | tf_op jit(solution)/shard_map/all_to_all | solution.py:259
  456.9 10.9 %copy-start.41 = (pred[4,2]{0,1:T(4,128)(4,1)S(1)}, pred[4,2]{0,1:T(4,128)(4,1)}, u32[]{:S(2)}) copy-start(pred[4,2]{0,1:T(4,128)(4,1)} %copy-done.40) | copy-start | bytes 28
  484.8 4.7 copy-start.4
  484.8 4.7 copy-start.38
  (26 other events, 62.0 us)
Sparse Core Ops, SparseCore 0:
  25.9 48.8 all-gather.4
  78.1 47.2 all-gather.6
  167.8 149.5 all-gather.8
  396.2 41.8 reduce-scatter.3
